TPU v7x, 512 devices: a whole 4x8x8 slice. The times are simulated.
512 devices in a mesh: section: 8 (over x, core), dp: 64 (over z, y).
Axes of the slice: x: 4, y: 8, z: 8, core: 2. Of those that a mesh axis runs over, the one named last changes fastest.
Arguments:
- inputs: bfloat16 [8, 1024, 4096], P(None, 'dp')
- cotangent: bfloat16 [8, 1024, 4096], P(None, 'dp'), may hold values from -0.59765625 to 0.59765625
- row_adapter_slot: int32 [8, 1024], P(None, 'dp'), may hold values from 0 to 1
- deployed_adapter_ids: int32 [64, 2], replicated, may hold values from 0 to 63, as said below
- adapter_owner_device: int32 [64], replicated, may hold values from 0 to 63, each once
- adapter_down_weight: bfloat16 [8, 1, 64, 2, 32, 4096], P('section', None, 'dp'), as said below
- adapter_up_weight: bfloat16 [8, 1, 64, 2, 32, 4096], P('section', None, 'dp'), as said below
Outputs:
- grad_down: float32 [8, 1, 64, 32, 4096], P('section', None, 'dp')
- grad_up: float32 [8, 1, 64, 32, 4096], P('section', None, 'dp')
Inputs may be any that keep to these rules, and one draw needn't show every extreme that they name: `deployed_adapter_ids`: the 2 adapter ids of one device differ, and every adapter is deployed on at least one device; some adapters are deployed on many devices. `adapter_owner_device`: every data device owns exactly one adapter. `adapter_down_weight`: copies of the same adapter on different devices are equal. `adapter_up_weight`: copies of the same adapter on different devices are equal.
All inputs are finite; a program needn't handle non-finite values.
Results may differ from a plain program's by a relative error of at most 0.0086.
Values may be sent and summed in bfloat16 or wider, within the bound.
A program may use at most 64 MiB of HBM per device.

v0:
```python
import jax
import jax.numpy as jnp
from jax import lax
from jax.sharding import PartitionSpec as P

adapter_scale = 0.5
epsilon = 1e-06


def from_behind(block, axis, distance):
    devices = range(lax.axis_size(axis))
    route = [(i - distance, i) for i in devices if i - distance in devices]
    return lax.ppermute(block, axis, route)


def norm_parts(hidden_state):
    value_rows = hidden_state.astype(jnp.float32)
    inverse = lax.rsqrt(jnp.mean(value_rows * value_rows, axis=-1, keepdims=True) + epsilon)
    return (inverse, value_rows * inverse)


def layer_forward(hidden_state, down_weight, up_weight, row_mask):
    inverse, unit = norm_parts(hidden_state)
    normed = unit.astype(jnp.bfloat16)
    rank_complete = lax.dot_general(
        normed, down_weight, (((1,), (1,)), ((), ())), preferred_element_type=jnp.float32
    )
    rank_row_values = jnp.where(row_mask, rank_complete, 0.0).astype(jnp.bfloat16)
    row_updates = jnp.dot(rank_row_values, up_weight, preferred_element_type=jnp.float32)
    return (
        (hidden_state.astype(jnp.float32) + adapter_scale * row_updates).astype(jnp.bfloat16),
        rank_row_values,
    )


def layer_backward(hidden_state, grad_rows, down_weight, up_weight, row_mask):
    inverse, unit = norm_parts(hidden_state)
    normed = unit.astype(jnp.bfloat16)
    rank_complete = adapter_scale * lax.dot_general(
        grad_rows, up_weight, (((1,), (1,)), ((), ())), preferred_element_type=jnp.float32
    )
    rank_grads = jnp.where(row_mask, rank_complete, 0.0).astype(jnp.bfloat16)
    unit_grads = jnp.dot(rank_grads, down_weight, preferred_element_type=jnp.float32)
    back_rows = grad_rows.astype(jnp.float32) + inverse * (
        unit_grads - unit * jnp.mean(unit_grads * unit, axis=-1, keepdims=True)
    )
    return (back_rows.astype(jnp.bfloat16), normed, rank_grads)


def put_block(store, layer_idx, position, value, usable):
    previous = store[layer_idx, position]
    return store.at[layer_idx, position].set(jnp.where(usable, value, previous))


def body(
    inputs,
    cotangent,
    row_adapter_slot,
    deployed_adapter_ids,
    adapter_owner_device,
    adapter_down_weight,
    adapter_up_weight,
):
    sections = lax.axis_size("section")
    section_index = lax.axis_index("section")
    pieces = lax.axis_size("dp")
    micro_count, row_count, feature_rows = inputs.shape
    layer_stack = adapter_down_weight.shape[1]
    adapter_slot_count = adapter_down_weight.shape[3]
    rank_length = adapter_down_weight.shape[4]
    rank_columns = adapter_slot_count * rank_length
    piece_cols = feature_rows // pieces
    down_weight = adapter_down_weight.reshape(layer_stack, rank_columns, feature_rows)
    up_weight = adapter_up_weight.reshape(layer_stack, rank_columns, feature_rows)
    column_slot = jnp.arange(rank_columns, dtype=jnp.int32) // rank_length
    masks = row_adapter_slot[..., None] == column_slot
    step_count = micro_count + sections - 1
    ticks = jnp.arange(step_count, dtype=jnp.int32)

    def forward_tick(carried, tick_now):
        incoming, saved_in, saved_rank = carried
        micro_index = tick_now - section_index
        usable = (micro_index >= 0) & (micro_index < micro_count)
        position = jnp.clip(micro_index, 0, micro_count - 1)
        hidden_state = jnp.where(section_index == 0, inputs[position], incoming)
        row_mask = masks[position]
        saved_in = put_block(saved_in, 0, position, hidden_state, usable)
        hidden_state, rank_row_values = layer_forward(
            hidden_state, down_weight[0], up_weight[0], row_mask
        )
        saved_rank = put_block(saved_rank, 0, position, rank_row_values, usable)
        incoming = from_behind(hidden_state, "section", 1)
        return ((incoming, saved_in, saved_rank), None)

    start_forward = (
        jnp.zeros((row_count, feature_rows), jnp.bfloat16),
        jnp.zeros((layer_stack, micro_count, row_count, feature_rows), jnp.bfloat16),
        jnp.zeros((layer_stack, micro_count, row_count, rank_columns), jnp.bfloat16),
    )
    (unused_rows, saved_in, saved_rank), unused_out = lax.scan(forward_tick, start_forward, ticks)
    records = (
        jnp.zeros((layer_stack, micro_count, row_count, feature_rows), jnp.bfloat16),
        jnp.zeros((layer_stack, micro_count, row_count, rank_columns), jnp.bfloat16),
    )

    def backward_tick(carried, tick_now):
        incoming, records = carried
        micro_index = tick_now - (sections - 1 - section_index)
        usable = (micro_index >= 0) & (micro_index < micro_count)
        position = jnp.clip(micro_index, 0, micro_count - 1)
        grad_rows = jnp.where(section_index == sections - 1, cotangent[position], incoming)
        row_mask = masks[position]
        for layer_idx in reversed(range(layer_stack)):
            hidden_state = saved_in[layer_idx, position]
            rank_row_values = saved_rank[layer_idx, position]
            back_rows, normed, rank_grads = layer_backward(
                hidden_state, grad_rows, down_weight[layer_idx], up_weight[layer_idx], row_mask
            )
            records = (
                put_block(records[0], layer_idx, position, grad_rows, usable),
                put_block(records[1], layer_idx, position, rank_grads, usable),
            )
            grad_rows = back_rows
        incoming = from_behind(grad_rows, "section", -1)
        return ((incoming, records), None)

    start_backward = (jnp.zeros((row_count, feature_rows), jnp.bfloat16), records)
    (unused_grads, records), unused_out = lax.scan(backward_tick, start_backward, ticks)
    token_count = micro_count * row_count
    normed_all = (
        norm_parts(saved_in)[1]
        .astype(jnp.bfloat16)
        .reshape(layer_stack, token_count, pieces, piece_cols)
    )
    grads_all = records[0].reshape(layer_stack, token_count, pieces, piece_cols)
    normed_recv, grads_recv = (
        lax.all_to_all(normed_all, "dp", split_axis=2, concat_axis=1, tiled=True),
        lax.all_to_all(grads_all, "dp", split_axis=2, concat_axis=1, tiled=True),
    )
    normed_recv = normed_recv.reshape(layer_stack, pieces, token_count, piece_cols)
    grads_recv = grads_recv.reshape(layer_stack, pieces, token_count, piece_cols)
    rank_local = saved_rank.reshape(layer_stack, token_count, rank_columns)
    rank_grad_local = records[1].reshape(layer_stack, token_count, rank_columns)
    rank_every, rank_grad_every = (
        lax.all_gather(rank_local, "dp", axis=1, tiled=True),
        lax.all_gather(rank_grad_local, "dp", axis=1, tiled=True),
    )
    rank_every = rank_every.reshape(layer_stack, pieces, token_count, rank_columns)
    rank_grad_every = rank_grad_every.reshape(layer_stack, pieces, token_count, rank_columns)
    pieces_down = jnp.einsum(
        "lstk,lstc->slkc", rank_grad_every, normed_recv, preferred_element_type=jnp.float32
    )
    up_gradient_pieces = adapter_scale * jnp.einsum(
        "lstk,lstc->slkc", rank_every, grads_recv, preferred_element_type=jnp.float32
    )
    pieces_down = pieces_down.reshape(
        pieces, layer_stack, adapter_slot_count, rank_length * piece_cols
    )
    up_gradient_pieces = up_gradient_pieces.reshape(
        pieces, layer_stack, adapter_slot_count, rank_length * piece_cols
    )
    adapters = adapter_owner_device.shape[0]
    adapter_ids = jnp.arange(adapters, dtype=jnp.int32)
    owner_of = jnp.sum(
        jnp.where(deployed_adapter_ids[..., None] == adapter_ids, adapter_owner_device, 0), axis=-1
    )
    owner_ids = jnp.arange(pieces, dtype=jnp.int32)
    select = (owner_of[None, :, :] == owner_ids[:, None, None]).astype(jnp.float32)
    owned_down = jnp.einsum("osk,slkx->olx", select, pieces_down, precision=lax.Precision.HIGHEST)
    owned_up = jnp.einsum(
        "osk,slkx->olx", select, up_gradient_pieces, precision=lax.Precision.HIGHEST
    )
    owned_down = owned_down.reshape(pieces, layer_stack, rank_length, piece_cols)
    owned_up = owned_up.reshape(pieces, layer_stack, rank_length, piece_cols)
    final_down, final_up = (
        lax.all_to_all(
            owned_down.astype(jnp.bfloat16), "dp", split_axis=0, concat_axis=3, tiled=True
        ).astype(owned_down.dtype),
        lax.all_to_all(
            owned_up.astype(jnp.bfloat16), "dp", split_axis=0, concat_axis=3, tiled=True
        ).astype(owned_up.dtype),
    )
    grad_down = final_down.reshape(1, layer_stack, 1, rank_length, feature_rows)
    grad_up = final_up.reshape(1, layer_stack, 1, rank_length, feature_rows)
    return (grad_down, grad_up)


def solution(mesh):
    placed = (
        P(None, "dp", None),
        P(None, "dp", None),
        P(None, "dp"),
        P(),
        P(),
        P("section", None, "dp", None, None, None),
        P("section", None, "dp", None, None, None),
    )
    return jax.shard_map(
        body,
        mesh=mesh,
        in_specs=placed,
        out_specs=(P("section", None, "dp", None, None), P("section", None, "dp", None, None)),
        check_vma=False,
    )
```

profile of v0, /device:TPU:2, one launch (start us, length us, event | category | flops | bytes accessed | tf_op | source)
XLA Modules:
  0.0 656.7 jit_solution(1103574373725658941)
XLA Ops:
  8.2 210.1 %while.35 = (s32[]{:T(128)}, bf16[16,4096]{1,0:T(8,128)(2,1)S(1)}, bf16[1,8,16,4096]{3,2,1,0:T(8,128)(2,1)S(1)}, bf16[1,8,16,64]{3,2,1,0:T(8,128)(2,1)S(1)}, pre...) while((s32[]{:T(128)}, bf16[16,4096]{1,0:T(8,128)(2,1)S(1)}, ...), condition=%wide.region_4.5_spmd, body=%wide.region_1.4_spmd.sunk | while | flops 17633332 | bytes 3036152 | solution.py:100
  17.8 4.4 collective-permute-done
  31.8 4.4 collective-permute-done
  45.9 4.4 collective-permute-done
  59.9 4.4 collective-permute-done
  73.9 4.4 collective-permute-done
  87.9 4.4 collective-permute-done
  101.9 4.4 collective-permute-done
  115.9 4.4 collective-permute-done
  129.9 4.4 collective-permute-done
  143.9 4.4 collective-permute-done
  157.9 4.4 collective-permute-done
  171.9 4.4 collective-permute-done
  199.9 4.4 collective-permute-done
  213.9 4.4 collective-permute-done
  218.4 192.8 %while.36 = (s32[]{:T(128)}, bf16[16,4096]{1,0:T(8,128)(2,1)S(1)}, bf16[1,8,16,4096]{3,2,1,0:T(8,128)(2,1)S(1)}, bf16[1,8,16,64]{3,2,1,0:T(8,128)(2,1)S(1)}, pre...) while((s32[]{:T(128)}, bf16[16,4096]{1,0:T(8,128)(2,1)S(1)}, ...), condition=%wide.region_9.10_spmd, body=%wide.region_5.9_spmd.sunk | while | flops 17962036 | bytes 5919656 | solution.py:128
  419.7 16.8 %all-to-all-start = ((bf16[1,128,64,64]{1,3,0,2:T(8,128)(2,1)}), bf16[1,128,64,64]{1,3,0,2:T(8,128)(2,1)}, u32[]{:S(2)}, u32[]{:S(2)}) async-start(bf16[1,128,64,64]{1,3,0,2:T(8,128)(2,1)} %copy.52), calls=%async_computation | async-start | bytes 2097152 | tf_op jit(solution)/shard_map/all_to_all | solution.py:137
  442.5 24.1 %all-to-all-done = bf16[1,128,64,64]{1,3,0,2:T(8,128)(2,1)} async-done(((bf16[1,128,64,64]{1,3,0,2:T(8,128)(2,1)}), bf16[1,128,64,64]{1,3,0,2:T(8,128)(2,1)}, u32[]{:S(2)}, u32[]{:S(2)}) %all-to-all-start) | async-done | bytes 1048608 | tf_op jit(solution)/shard_map/all_to_all | solution.py:137
  466.6 8.4 %all-to-all-start.2 = ((bf16[1,128,64,64]{1,3,0,2:T(8,128)(2,1)}), bf16[1,128,64,64]{1,3,0,2:T(8,128)(2,1)}, u32[]{:S(2)}, u32[]{:S(2)}) async-start(bf16[1,128,64,64]{1,3,0,2:T(8,128)(2,1)} %copy.59), calls=%async_computation.2 | async-start | bytes 2097152 | tf_op jit(solution)/shard_map/all_to_all | solution.py:138
  475.2 46.8 %all-gather.3.cloned.1.call-done = bf16[1,8192,64]{1,2,0:T(8,128)(2,1)} async-done(((bf16[1,128,64]{1,2,0:T(8,128)(2,1)}), bf16[1,8192,64]{1,2,0:T(8,128)(2,1)}) %all-gather.3.cloned.1.call-update) | async-done | bytes 1048592 | tf_op jit(solution)/shard_map/all_gather | solution.py:146
  534.0 67.8 %all-gather.5.cloned.1.call-done = bf16[1,8192,64]{1,2,0:T(8,128)(2,1)} async-done(((bf16[1,128,64]{1,2,0:T(8,128)(2,1)}), bf16[1,8192,64]{1,2,0:T(8,128)(2,1)}) %all-gather.5.cloned.1.call-update) | async-done | bytes 1048592 | tf_op jit(solution)/shard_map/all_gather | solution.py:145
  603.2 8.0 %all-to-all-start.1 = ((bf16[64,2,1024]{2,1,0:T(2,128)(2,1)}), bf16[64,2,1024]{2,1,0:T(2,128)(2,1)S(1)}, u32[]{:S(2)}, u32[]{:S(2)}) async-start(bf16[64,2,1024]{2,1,0:T(2,128)(2,1)} %reshape.335), calls=%async_computation.1 | async-start | bytes 524288 | tf_op jit(solution)/shard_map/all_to_all | solution.py:176
  624.6 9.5 %all-to-all-start.3 = ((bf16[64,2,1024]{2,1,0:T(2,128)(2,1)}), bf16[64,2,1024]{2,1,0:T(2,128)(2,1)S(1)}, u32[]{:S(2)}, u32[]{:S(2)}) async-start(bf16[64,2,1024]{2,1,0:T(2,128)(2,1)} %reshape.337), calls=%async_computation.3 | async-start | bytes 524288 | tf_op jit(solution)/shard_map/all_to_all | solution.py:179
  636.3 11.3 %all-to-all-done.3 = bf16[64,2,1024]{2,1,0:T(2,128)(2,1)S(1)} async-done(((bf16[64,2,1024]{2,1,0:T(2,128)(2,1)}), bf16[64,2,1024]{2,1,0:T(2,128)(2,1)S(1)}, u32[]{:S(2)}, u32[]{:S(2)}) %all-to-all-start.3) | async-done | bytes 262176 | tf_op jit(solution)/shard_map/all_to_all | solution.py:179
  (430 shorter events, 367.8 us)
Async XLA Ops:
  7.2 514.8 %all-gather.3.cloned.1.call-start = ((), (), s32[]{:S(2)}) async-start(), calls=%async_computation.4 | async-start | bytes 1064960 | tf_op jit(solution)/shard_map/all_gather | solution.py:146
  15.9 6.3 collective-permute-start
  29.9 6.4 collective-permute-start
  44.0 6.3 collective-permute-start
  58.0 6.3 collective-permute-start
  72.0 6.3 collective-permute-start
  236.2 6.3 collective-permute-start.1
  249.2 6.3 collective-permute-start.1
  262.2 6.3 collective-permute-start.1
  275.1 6.3 collective-permute-start.1
  288.1 6.3 collective-permute-start.1
  301.1 6.3 collective-permute-start.1
  314.1 6.3 collective-permute-start.1
  327.0 6.3 collective-permute-start.1
  353.0 6.3 collective-permute-start.1
  366.0 6.3 collective-permute-start.1
  378.9 6.3 collective-permute-start.1
  391.9 6.3 collective-permute-start.1
  404.9 6.3 collective-permute-start.1
  419.7 46.9 %all-to-all-start = ((bf16[1,128,64,64]{1,3,0,2:T(8,128)(2,1)}), bf16[1,128,64,64]{1,3,0,2:T(8,128)(2,1)}, u32[]{:S(2)}, u32[]{:S(2)}) async-start(bf16[1,128,64,64]{1,3,0,2:T(8,128)(2,1)} %copy.52), calls=%async_computation | async-start | bytes 2097152 | tf_op jit(solution)/shard_map/all_to_all | solution.py:137
  436.5 165.3 %all-gather.5.cloned.1.call-start = ((), (), s32[]{:S(2)}) async-start(), calls=%async_computation.5 | async-start | bytes 1064960 | tf_op jit(solution)/shard_map/all_gather | solution.py:145
  466.6 136.7 %all-to-all-start.2 = ((bf16[1,128,64,64]{1,3,0,2:T(8,128)(2,1)}), bf16[1,128,64,64]{1,3,0,2:T(8,128)(2,1)}, u32[]{:S(2)}, u32[]{:S(2)}) async-start(bf16[1,128,64,64]{1,3,0,2:T(8,128)(2,1)} %copy.59), calls=%async_computation.2 | async-start | bytes 2097152 | tf_op jit(solution)/shard_map/all_to_all | solution.py:138
  603.2 21.4 %all-to-all-start.1 = ((bf16[64,2,1024]{2,1,0:T(2,128)(2,1)}), bf16[64,2,1024]{2,1,0:T(2,128)(2,1)S(1)}, u32[]{:S(2)}, u32[]{:S(2)}) async-start(bf16[64,2,1024]{2,1,0:T(2,128)(2,1)} %reshape.335), calls=%async_computation.1 | async-start | bytes 524288 | tf_op jit(solution)/shard_map/all_to_all | solution.py:176
  624.6 23.1 %all-to-all-start.3 = ((bf16[64,2,1024]{2,1,0:T(2,128)(2,1)}), bf16[64,2,1024]{2,1,0:T(2,128)(2,1)S(1)}, u32[]{:S(2)}, u32[]{:S(2)}) async-start(bf16[64,2,1024]{2,1,0:T(2,128)(2,1)} %reshape.337), calls=%async_computation.3 | async-start | bytes 524288 | tf_op jit(solution)/shard_map/all_to_all | solution.py:179
  (29 other events, 237.7 us)
Sparse Core Ops, SparseCore 0:
  412.0 109.9 all-gather.2
  525.5 76.1 all-gather.4
where the time goes:
time: 662 us; the launch traced here: 657 us
  waiting for transfers between devices  256 us (39%)
  starting transfers between devices  126 us (19%)
  other arithmetic  98.3 us (15%)
  matrix products  89.6 us (14%)
  local copies, waits for them, and re-layouts  51.3 us (8%)
  loops' own time  21 us (3%)
  between operations  14.3 us (2%)
    ppermute x30, waiting for transfers between devices, from_behind(): return lax.ppermute(block, axis, route)  103 us
    ppermute x30, starting transfers between devices, from_behind(): return lax.ppermute(block, axis, route)  83.7 us
    all_gather x1, waiting for transfers between devices, body(): lax.all_gather(rank_local, 'dp', axis=1, tiled=True)  67.8 us
    scatter x30, other arithmetic, put_block(): return store.at[layer_idx, position].set(jnp.where(usable, value, previous))  47 us
    all_gather x1, waiting for transfers between devices, body(): lax.all_gather(rank_grad_local, 'dp', axis=1, tiled=True)  46.8 us
    another operation x30, other arithmetic  41.5 us
    dot_general x15, matrix products, layer_forward(): lax.dot_general(normed, down_weight, (((1,), (1,)), ((), ())), preferred_...  29.6 us
    dot_general x15, matrix products, layer_backward(): lax.dot_general(grad_rows, up_weight, (((1,), (1,)), ((), ())), preferred...  27.9 us
  transfers between devices with their start and end apart: 36, of which 35 were waited for; matrix products, arithmetic and copies ran while one was open for 6% of the time, Pallas kernels for 0%

commit v1 on v0

--- a/solution.py
+++ b/solution.py
@@ -61,6 +61,12 @@
     adapter_down_weight,
     adapter_up_weight,
 ):
+
+    def fields_balance(mine_x):
+        raw_out = jnp.stack([mine_x for _ in range(lax.axis_size("dp"))], 0)
+        base_arr = lax.all_to_all(raw_out, "dp", 0, 0)
+        return jnp.concatenate(base_arr, 1)
+
     sections = lax.axis_size("section")
     section_index = lax.axis_index("section")
     pieces = lax.axis_size("dp")
@@ -143,7 +149,7 @@
     rank_grad_local = records[1].reshape(layer_stack, token_count, rank_columns)
     rank_every, rank_grad_every = (
         lax.all_gather(rank_local, "dp", axis=1, tiled=True),
-        lax.all_gather(rank_grad_local, "dp", axis=1, tiled=True),
+        fields_balance(rank_grad_local),
     )
     rank_every = rank_every.reshape(layer_stack, pieces, token_count, rank_columns)
     rank_grad_every = rank_grad_every.reshape(layer_stack, pieces, token_count, rank_columns)

time: 662 us -> 591 us (0.89)
  waiting for transfers between devices: 256 us -> 196 us
  matrix products: 89.6 us -> 75.6 us
  starting transfers between devices: 126 us -> 140 us
  other arithmetic: 98.3 us -> 89.9 us
    all_gather x1 -> x0, waiting for transfers between devices: 46.8 us -> none  [body(): lax.all_gather(rank_grad_local, 'dp', axis=1, tiled=True)]
    all_to_all x1, waiting for transfers between devices: 24.1 us -> 0.01 us  [body(): lax.all_to_all(normed_all, 'dp', split_axis=2, concat_axis=1, tiled=True)]
    all_to_all x0 -> x1, waiting for transfers between devices: none -> 23.6 us  [fields_balance(): base_arr = lax.all_to_all(raw_out, 'dp', 0, 0)]
    dot_general x15, matrix products: 27.9 us -> 13.1 us  [layer_backward(): lax.dot_general(grad_rows, up_weight, (((1,), (1,)), ((), ())), preferred...]
    all_gather x1, waiting for transfers between devices: 67.8 us -> 54.8 us  [body(): lax.all_gather(rank_local, 'dp', axis=1, tiled=True)]
    all_to_all x0 -> x1, starting transfers between devices: none -> 12.9 us  [fields_balance(): base_arr = lax.all_to_all(raw_out, 'dp', 0, 0)]
    another operation x30, other arithmetic: 41.5 us -> 32.6 us
  transfers between devices with their start and end apart: 36 -> 36, of which waited for: 35 -> 34; matrix products, arithmetic and copies ran while one was open for 6% -> 17% of each run, Pallas kernels for 0% -> 0%
where the time goes in v1:
time: 591 us; the launch traced here: 586 us
  waiting for transfers between devices  196 us (33%)
  starting transfers between devices  140 us (24%)
  other arithmetic  89.9 us (15%)
  matrix products  75.6 us (13%)
  local copies, waits for them, and re-layouts  51.5 us (9%)
  loops' own time  19.4 us (3%)
  between operations  14.4 us (2%)
    ppermute x30, waiting for transfers between devices, from_behind(): return lax.ppermute(block, axis, route)  103 us
    ppermute x30, starting transfers between devices, from_behind(): return lax.ppermute(block, axis, route)  84 us
    all_gather x1, waiting for transfers between devices, body(): lax.all_gather(rank_local, 'dp', axis=1, tiled=True)  54.8 us
    scatter x30, other arithmetic, put_block(): return store.at[layer_idx, position].set(jnp.where(usable, value, previous))  48.5 us
    another operation x30, other arithmetic  32.6 us
    dot_general x15, matrix products, layer_forward(): lax.dot_general(normed, down_weight, (((1,), (1,)), ((), ())), preferred_...  30.3 us
    all_to_all x1, waiting for transfers between devices, fields_balance(): base_arr = lax.all_to_all(raw_out, 'dp', 0, 0)  23.6 us
    dot_general x15, matrix products, layer_forward(): jnp.dot(rank_row_values, up_weight, preferred_element_type=jnp.float32)  18.8 us
  transfers between devices with their start and end apart: 36, of which 34 were waited for; matrix products, arithmetic and copies ran while one was open for 17% of the time, Pallas kernels for 0%

profile of v1, /device:TPU:2, one launch (start us, length us, event | category | flops | bytes accessed | tf_op | source)
XLA Modules:
  0.0 586.4 jit_solution(15111999495730066679)
XLA Ops:
  8.1 210.2 %while.35 = (s32[]{:T(128)}, bf16[16,4096]{1,0:T(8,128)(2,1)S(1)}, bf16[1,8,16,4096]{3,2,1,0:T(8,128)(2,1)S(1)}, bf16[1,8,16,64]{3,2,1,0:T(8,128)(2,1)S(1)}, pre...) while((s32[]{:T(128)}, bf16[16,4096]{1,0:T(8,128)(2,1)S(1)}, ...), condition=%wide.region_4.5_spmd, body=%wide.region_1.4_spmd.sunk | while | flops 17633332 | bytes 3036152 | solution.py:106
  17.8 4.4 collective-permute-done
  31.8 4.4 collective-permute-done
  45.9 4.4 collective-permute-done
  59.9 4.4 collective-permute-done
  73.9 4.4 collective-permute-done
  87.9 4.4 collective-permute-done
  101.9 4.4 collective-permute-done
  115.9 4.4 collective-permute-done
  143.9 4.4 collective-permute-done
  157.9 4.4 collective-permute-done
  171.9 4.4 collective-permute-done
  185.9 4.4 collective-permute-done
  199.9 4.4 collective-permute-done
  214.0 4.4 collective-permute-done
  226.3 16.9 %all-to-all-start.1 = ((bf16[1,128,64,64]{1,3,0,2:T(8,128)(2,1)}), bf16[1,128,64,64]{1,3,0,2:T(8,128)(2,1)}, u32[]{:S(2)}, u32[]{:S(2)}) async-start(bf16[1,128,64,64]{1,3,0,2:T(8,128)(2,1)} %copy.50), calls=%async_computation.1 | async-start | bytes 2097152 | tf_op jit(solution)/shard_map/all_to_all | solution.py:143
  243.3 170.2 %while.36 = (s32[]{:T(128)}, bf16[16,4096]{1,0:T(8,128)(2,1)S(1)}, bf16[1,8,16,4096]{3,2,1,0:T(8,128)(2,1)S(1)}, bf16[1,8,16,64]{3,2,1,0:T(8,128)(2,1)S(1)}, pre...) while((s32[]{:T(128)}, bf16[16,4096]{1,0:T(8,128)(2,1)S(1)}, ...), condition=%wide.region_9.10_spmd, body=%wide.region_5.9_spmd.sunk | while | flops 17962036 | bytes 3822476 | solution.py:134
  414.9 12.9 %all-to-all-start = ((bf16[64,1,128,64]{2,3,1,0:T(8,128)(2,1)}), bf16[64,1,128,64]{2,3,1,0:T(8,128)(2,1)}, u32[]{:S(2)}, u32[]{:S(2)}) async-start(bf16[64,1,128,64]{2,3,1,0:T(8,128)(2,1)} %stack.3), calls=%async_computation | async-start | bytes 2097152 | tf_op jit(solution)/shard_map/all_to_all | solution.py:67
  433.9 23.6 %all-to-all-done = bf16[64,1,128,64]{2,3,1,0:T(8,128)(2,1)} async-done(((bf16[64,1,128,64]{2,3,1,0:T(8,128)(2,1)}), bf16[64,1,128,64]{2,3,1,0:T(8,128)(2,1)}, u32[]{:S(2)}, u32[]{:S(2)}) %all-to-all-start) | async-done | bytes 1048608 | tf_op jit(solution)/shard_map/all_to_all | solution.py:67
  457.5 8.6 %all-to-all-start.3 = ((bf16[1,128,64,64]{1,3,0,2:T(8,128)(2,1)}), bf16[1,128,64,64]{1,3,0,2:T(8,128)(2,1)}, u32[]{:S(2)}, u32[]{:S(2)}) async-start(bf16[1,128,64,64]{1,3,0,2:T(8,128)(2,1)} %copy.56), calls=%async_computation.3 | async-start | bytes 2097152 | tf_op jit(solution)/shard_map/all_to_all | solution.py:144
  476.6 54.8 %all-gather.2.cloned.1.call-done = bf16[1,8192,64]{1,2,0:T(8,128)(2,1)} async-done(((bf16[1,128,64]{1,2,0:T(8,128)(2,1)}), bf16[1,8192,64]{1,2,0:T(8,128)(2,1)}) %all-gather.2.cloned.1.call-update) | async-done | bytes 1048592 | tf_op jit(solution)/shard_map/all_gather | solution.py:151
  532.9 8.0 %all-to-all-start.2 = ((bf16[64,2,1024]{2,1,0:T(2,128)(2,1)}), bf16[64,2,1024]{2,1,0:T(2,128)(2,1)S(1)}, u32[]{:S(2)}, u32[]{:S(2)}) async-start(bf16[64,2,1024]{2,1,0:T(2,128)(2,1)} %reshape.335), calls=%async_computation.2 | async-start | bytes 524288 | tf_op jit(solution)/shard_map/all_to_all | solution.py:182
  554.3 9.5 %all-to-all-start.4 = ((bf16[64,2,1024]{2,1,0:T(2,128)(2,1)}), bf16[64,2,1024]{2,1,0:T(2,128)(2,1)S(1)}, u32[]{:S(2)}, u32[]{:S(2)}) async-start(bf16[64,2,1024]{2,1,0:T(2,128)(2,1)} %reshape.337), calls=%async_computation.4 | async-start | bytes 524288 | tf_op jit(solution)/shard_map/all_to_all | solution.py:185
  566.0 11.3 %all-to-all-done.4 = bf16[64,2,1024]{2,1,0:T(2,128)(2,1)S(1)} async-done(((bf16[64,2,1024]{2,1,0:T(2,128)(2,1)}), bf16[64,2,1024]{2,1,0:T(2,128)(2,1)S(1)}, u32[]{:S(2)}, u32[]{:S(2)}) %all-to-all-start.4) | async-done | bytes 262176 | tf_op jit(solution)/shard_map/all_to_all | solution.py:185
  (405 shorter events, 346.1 us)
Async XLA Ops:
  15.8 6.3 %collective-permute-start = (bf16[16,4096]{1,0:T(8,128)(2,1)S(1)}, bf16[16,4096]{1,0:T(8,128)(2,1)S(1)}, u32[]{:S(2)}, u32[]{:S(2)}) collective-permute-start(bf16[16,4096]{1,0:T(8,128)(2,1)S(1)} %fusion.84), channel_id=1, source_target_pairs={{0,64},{64,128},{128,192},{192,256},{256,320},{320,384},{384,448},... | collective-permute-start | bytes 393224 | tf_op jit(solution)/shard_map/while/body/eval_jaxpr/ppermute | solution.py:13
  29.9 6.4 %collective-permute-start = (bf16[16,4096]{1,0:T(8,128)(2,1)S(1)}, bf16[16,4096]{1,0:T(8,128)(2,1)S(1)}, u32[]{:S(2)}, u32[]{:S(2)}) collective-permute-start(bf16[16,4096]{1,0:T(8,128)(2,1)S(1)} %fusion.84), channel_id=1, source_target_pairs={{0,64},{64,128},{128,192},{192,256},{256,320},{320,384},{384,448},... | collective-permute-start | bytes 393224 | tf_op jit(solution)/shard_map/while/body/eval_jaxpr/ppermute | solution.py:13
  44.0 6.3 %collective-permute-start = (bf16[16,4096]{1,0:T(8,128)(2,1)S(1)}, bf16[16,4096]{1,0:T(8,128)(2,1)S(1)}, u32[]{:S(2)}, u32[]{:S(2)}) collective-permute-start(bf16[16,4096]{1,0:T(8,128)(2,1)S(1)} %fusion.84), channel_id=1, source_target_pairs={{0,64},{64,128},{128,192},{192,256},{256,320},{320,384},{384,448},... | collective-permute-start | bytes 393224 | tf_op jit(solution)/shard_map/while/body/eval_jaxpr/ppermute | solution.py:13
  212.0 6.3 %collective-permute-start = (bf16[16,4096]{1,0:T(8,128)(2,1)S(1)}, bf16[16,4096]{1,0:T(8,128)(2,1)S(1)}, u32[]{:S(2)}, u32[]{:S(2)}) collective-permute-start(bf16[16,4096]{1,0:T(8,128)(2,1)S(1)} %fusion.84), channel_id=1, source_target_pairs={{0,64},{64,128},{128,192},{192,256},{256,320},{320,384},{384,448},... | collective-permute-start | bytes 393224 | tf_op jit(solution)/shard_map/while/body/eval_jaxpr/ppermute | solution.py:13
  226.3 187.4 %all-to-all-start.1 = ((bf16[1,128,64,64]{1,3,0,2:T(8,128)(2,1)}), bf16[1,128,64,64]{1,3,0,2:T(8,128)(2,1)}, u32[]{:S(2)}, u32[]{:S(2)}) async-start(bf16[1,128,64,64]{1,3,0,2:T(8,128)(2,1)} %copy.50), calls=%async_computation.1 | async-start | bytes 2097152 | tf_op jit(solution)/shard_map/all_to_all | solution.py:143
  258.1 6.7 %collective-permute-start.1 = (bf16[16,4096]{1,0:T(8,128)(2,1)S(1)}, bf16[16,4096]{1,0:T(8,128)(2,1)S(1)}, u32[]{:S(2)}, u32[]{:S(2)}) collective-permute-start(bf16[16,4096]{1,0:T(8,128)(2,1)S(1)} %fusion.93), channel_id=1, source_target_pairs={{64,0},{128,64},{192,128},{256,192},{320,256},{384,320},{448,384},... | collective-permute-start | bytes 393224 | tf_op jit(solution)/shard_map/while/body/eval_jaxpr/ppermute | solution.py:13
  269.9 6.3 %collective-permute-start.1 = (bf16[16,4096]{1,0:T(8,128)(2,1)S(1)}, bf16[16,4096]{1,0:T(8,128)(2,1)S(1)}, u32[]{:S(2)}, u32[]{:S(2)}) collective-permute-start(bf16[16,4096]{1,0:T(8,128)(2,1)S(1)} %fusion.93), channel_id=1, source_target_pairs={{64,0},{128,64},{192,128},{256,192},{320,256},{384,320},{448,384},... | collective-permute-start | bytes 393224 | tf_op jit(solution)/shard_map/while/body/eval_jaxpr/ppermute | solution.py:13
  281.4 6.3 %collective-permute-start.1 = (bf16[16,4096]{1,0:T(8,128)(2,1)S(1)}, bf16[16,4096]{1,0:T(8,128)(2,1)S(1)}, u32[]{:S(2)}, u32[]{:S(2)}) collective-permute-start(bf16[16,4096]{1,0:T(8,128)(2,1)S(1)} %fusion.93), channel_id=1, source_target_pairs={{64,0},{128,64},{192,128},{256,192},{320,256},{384,320},{448,384},... | collective-permute-start | bytes 393224 | tf_op jit(solution)/shard_map/while/body/eval_jaxpr/ppermute | solution.py:13
  292.8 6.3 %collective-permute-start.1 = (bf16[16,4096]{1,0:T(8,128)(2,1)S(1)}, bf16[16,4096]{1,0:T(8,128)(2,1)S(1)}, u32[]{:S(2)}, u32[]{:S(2)}) collective-permute-start(bf16[16,4096]{1,0:T(8,128)(2,1)S(1)} %fusion.93), channel_id=1, source_target_pairs={{64,0},{128,64},{192,128},{256,192},{320,256},{384,320},{448,384},... | collective-permute-start | bytes 393224 | tf_op jit(solution)/shard_map/while/body/eval_jaxpr/ppermute | solution.py:13
  304.3 6.3 %collective-permute-start.1 = (bf16[16,4096]{1,0:T(8,128)(2,1)S(1)}, bf16[16,4096]{1,0:T(8,128)(2,1)S(1)}, u32[]{:S(2)}, u32[]{:S(2)}) collective-permute-start(bf16[16,4096]{1,0:T(8,128)(2,1)S(1)} %fusion.93), channel_id=1, source_target_pairs={{64,0},{128,64},{192,128},{256,192},{320,256},{384,320},{448,384},... | collective-permute-start | bytes 393224 | tf_op jit(solution)/shard_map/while/body/eval_jaxpr/ppermute | solution.py:13
  315.7 6.3 %collective-permute-start.1 = (bf16[16,4096]{1,0:T(8,128)(2,1)S(1)}, bf16[16,4096]{1,0:T(8,128)(2,1)S(1)}, u32[]{:S(2)}, u32[]{:S(2)}) collective-permute-start(bf16[16,4096]{1,0:T(8,128)(2,1)S(1)} %fusion.93), channel_id=1, source_target_pairs={{64,0},{128,64},{192,128},{256,192},{320,256},{384,320},{448,384},... | collective-permute-start | bytes 393224 | tf_op jit(solution)/shard_map/while/body/eval_jaxpr/ppermute | solution.py:13
  327.2 6.3 %collective-permute-start.1 = (bf16[16,4096]{1,0:T(8,128)(2,1)S(1)}, bf16[16,4096]{1,0:T(8,128)(2,1)S(1)}, u32[]{:S(2)}, u32[]{:S(2)}) collective-permute-start(bf16[16,4096]{1,0:T(8,128)(2,1)S(1)} %fusion.93), channel_id=1, source_target_pairs={{64,0},{128,64},{192,128},{256,192},{320,256},{384,320},{448,384},... | collective-permute-start | bytes 393224 | tf_op jit(solution)/shard_map/while/body/eval_jaxpr/ppermute | solution.py:13
  338.6 6.3 %collective-permute-start.1 = (bf16[16,4096]{1,0:T(8,128)(2,1)S(1)}, bf16[16,4096]{1,0:T(8,128)(2,1)S(1)}, u32[]{:S(2)}, u32[]{:S(2)}) collective-permute-start(bf16[16,4096]{1,0:T(8,128)(2,1)S(1)} %fusion.93), channel_id=1, source_target_pairs={{64,0},{128,64},{192,128},{256,192},{320,256},{384,320},{448,384},... | collective-permute-start | bytes 393224 | tf_op jit(solution)/shard_map/while/body/eval_jaxpr/ppermute | solution.py:13
  350.1 6.3 %collective-permute-start.1 = (bf16[16,4096]{1,0:T(8,128)(2,1)S(1)}, bf16[16,4096]{1,0:T(8,128)(2,1)S(1)}, u32[]{:S(2)}, u32[]{:S(2)}) collective-permute-start(bf16[16,4096]{1,0:T(8,128)(2,1)S(1)} %fusion.93), channel_id=1, source_target_pairs={{64,0},{128,64},{192,128},{256,192},{320,256},{384,320},{448,384},... | collective-permute-start | bytes 393224 | tf_op jit(solution)/shard_map/while/body/eval_jaxpr/ppermute | solution.py:13
  361.5 6.3 %collective-permute-start.1 = (bf16[16,4096]{1,0:T(8,128)(2,1)S(1)}, bf16[16,4096]{1,0:T(8,128)(2,1)S(1)}, u32[]{:S(2)}, u32[]{:S(2)}) collective-permute-start(bf16[16,4096]{1,0:T(8,128)(2,1)S(1)} %fusion.93), channel_id=1, source_target_pairs={{64,0},{128,64},{192,128},{256,192},{320,256},{384,320},{448,384},... | collective-permute-start | bytes 393224 | tf_op jit(solution)/shard_map/while/body/eval_jaxpr/ppermute | solution.py:13
  373.0 6.3 %collective-permute-start.1 = (bf16[16,4096]{1,0:T(8,128)(2,1)S(1)}, bf16[16,4096]{1,0:T(8,128)(2,1)S(1)}, u32[]{:S(2)}, u32[]{:S(2)}) collective-permute-start(bf16[16,4096]{1,0:T(8,128)(2,1)S(1)} %fusion.93), channel_id=1, source_target_pairs={{64,0},{128,64},{192,128},{256,192},{320,256},{384,320},{448,384},... | collective-permute-start | bytes 393224 | tf_op jit(solution)/shard_map/while/body/eval_jaxpr/ppermute | solution.py:13
  384.4 6.3 %collective-permute-start.1 = (bf16[16,4096]{1,0:T(8,128)(2,1)S(1)}, bf16[16,4096]{1,0:T(8,128)(2,1)S(1)}, u32[]{:S(2)}, u32[]{:S(2)}) collective-permute-start(bf16[16,4096]{1,0:T(8,128)(2,1)S(1)} %fusion.93), channel_id=1, source_target_pairs={{64,0},{128,64},{192,128},{256,192},{320,256},{384,320},{448,384},... | collective-permute-start | bytes 393224 | tf_op jit(solution)/shard_map/while/body/eval_jaxpr/ppermute | solution.py:13
  395.8 6.3 %collective-permute-start.1 = (bf16[16,4096]{1,0:T(8,128)(2,1)S(1)}, bf16[16,4096]{1,0:T(8,128)(2,1)S(1)}, u32[]{:S(2)}, u32[]{:S(2)}) collective-permute-start(bf16[16,4096]{1,0:T(8,128)(2,1)S(1)} %fusion.93), channel_id=1, source_target_pairs={{64,0},{128,64},{192,128},{256,192},{320,256},{384,320},{448,384},... | collective-permute-start | bytes 393224 | tf_op jit(solution)/shard_map/while/body/eval_jaxpr/ppermute | solution.py:13
  407.3 6.3 %collective-permute-start.1 = (bf16[16,4096]{1,0:T(8,128)(2,1)S(1)}, bf16[16,4096]{1,0:T(8,128)(2,1)S(1)}, u32[]{:S(2)}, u32[]{:S(2)}) collective-permute-start(bf16[16,4096]{1,0:T(8,128)(2,1)S(1)} %fusion.93), channel_id=1, source_target_pairs={{64,0},{128,64},{192,128},{256,192},{320,256},{384,320},{448,384},... | collective-permute-start | bytes 393224 | tf_op jit(solution)/shard_map/while/body/eval_jaxpr/ppermute | solution.py:13
  414.9 42.6 %all-to-all-start = ((bf16[64,1,128,64]{2,3,1,0:T(8,128)(2,1)}), bf16[64,1,128,64]{2,3,1,0:T(8,128)(2,1)}, u32[]{:S(2)}, u32[]{:S(2)}) async-start(bf16[64,1,128,64]{2,3,1,0:T(8,128)(2,1)} %stack.3), calls=%async_computation | async-start | bytes 2097152 | tf_op jit(solution)/shard_map/all_to_all | solution.py:67
  427.8 103.6 %all-gather.2.cloned.1.call-start = ((), (), s32[]{:S(2)}) async-start(), calls=%async_computation.5 | async-start | bytes 1064960 | tf_op jit(solution)/shard_map/all_gather | solution.py:151
  457.5 75.4 %all-to-all-start.3 = ((bf16[1,128,64,64]{1,3,0,2:T(8,128)(2,1)}), bf16[1,128,64,64]{1,3,0,2:T(8,128)(2,1)}, u32[]{:S(2)}, u32[]{:S(2)}) async-start(bf16[1,128,64,64]{1,3,0,2:T(8,128)(2,1)} %copy.56), calls=%async_computation.3 | async-start | bytes 2097152 | tf_op jit(solution)/shard_map/all_to_all | solution.py:144
  532.9 21.4 %all-to-all-start.2 = ((bf16[64,2,1024]{2,1,0:T(2,128)(2,1)}), bf16[64,2,1024]{2,1,0:T(2,128)(2,1)S(1)}, u32[]{:S(2)}, u32[]{:S(2)}) async-start(bf16[64,2,1024]{2,1,0:T(2,128)(2,1)} %reshape.335), calls=%async_computation.2 | async-start | bytes 524288 | tf_op jit(solution)/shard_map/all_to_all | solution.py:182
  554.3 23.1 %all-to-all-start.4 = ((bf16[64,2,1024]{2,1,0:T(2,128)(2,1)}), bf16[64,2,1024]{2,1,0:T(2,128)(2,1)S(1)}, u32[]{:S(2)}, u32[]{:S(2)}) async-start(bf16[64,2,1024]{2,1,0:T(2,128)(2,1)} %reshape.337), calls=%async_computation.4 | async-start | bytes 524288 | tf_op jit(solution)/shard_map/all_to_all | solution.py:185
  (17 other events, 195.2 us)
Sparse Core Ops, SparseCore 0:
  432.2 99.1 all-gather.1
